TPU v7x, 128 devices: a whole 4x4x4 slice. The times are simulated.
128 devices in a mesh: row: 16 (over x, z), col: 8 (over y, core).
Axes of the slice: x: 4, y: 4, z: 4, core: 2. Of those that a mesh axis runs over, the one named last changes fastest.
Arguments:
- diag_one: float32 [512, 512], P('row')
- coupling: float32 [512, 512], P('row'), may hold values from -0.25 to 0.25
- diag_two: float32 [512, 512], P('row')
- off_one: float32 [32768, 512], P(('row', 'col')), may hold values from -2 to 2
- off_two: float32 [32768, 512], P(('row', 'col')), may hold values from -2 to 2
- targets: float32 [16384, 128, 128], P(('row', 'col')), may hold values from -6 to 6
- pattern: int32 [16384, 2], P(('row', 'col')), may hold values from 0 to 255, as said below
Outputs:
- lower_one: float32 [32768, 512], P(('row', 'col'))
- lower_two: float32 [32768, 512], P(('row', 'col'))
- updated: float32 [16384, 128, 128], P(('row', 'col'))
Inputs may be any that keep to these rules, and one draw needn't show every extreme that they name: Rows of pattern come in groups of 128; group f belongs to grid position (r, c) = (f // 8, f % 8) of the row and col axes (sizes 16, 8). Its block rows i lie in r * 8 * 2 to (r + 1) * 8 * 2 - 1; its block columns j satisfy (j // 2) % 8 == c; always j <= i. Pairs may repeat.
All inputs are finite; a program needn't handle non-finite values.
Results may differ from a plain program's by a relative error of at most 0.00005.
Values sent between devices are 32-bit elements; how exact they have to be, the bound alone decides.
No kernel may reach another device: no remote copies, remote signals or barrier semaphores. Data moves between devices by JAX's collectives and lax.ppermute only.
A program may use at most 128 MiB of HBM per device.

v0:
```python
import jax
import jax.numpy as jnp
from jax import lax
from jax.sharding import PartitionSpec as P


def make_solver(chol):

    def apply_solve(rows):
        return lax.linalg.triangular_solve(
            chol, rows, left_side=False, lower=True, transpose_a=True
        )

    return apply_solve


def pair_updates(targets, pattern, row_one, row_two, col_one, col_two, shard_blocks):
    highest = lax.Precision.HIGHEST
    block = targets.shape[1]
    width = row_one.shape[1]
    ncol = lax.axis_size("col")
    span = row_one.shape[0] // block
    row_blocks_one = row_one.reshape(span, block, width)
    row_blocks_two = row_two.reshape(span, block, width)
    col_span = col_one.shape[0] // block
    col_blocks_one = col_one.reshape(col_span, block, width)
    col_blocks_two = col_two.reshape(col_span, block, width)
    local_row = pattern[:, 0] % span
    global_col = pattern[:, 1]
    local_col = global_col // (shard_blocks * ncol) * shard_blocks + global_col % shard_blocks
    groups = targets.shape[0] // 16
    tiles = targets.reshape(groups, 16, block, block)

    def one_group(items):
        tile, row_id, col_id = items
        first = jnp.einsum(
            "kaw,kbw->kab", row_blocks_one[row_id], col_blocks_one[col_id], precision=highest
        )
        second = jnp.einsum(
            "kaw,kbw->kab", row_blocks_two[row_id], col_blocks_two[col_id], precision=highest
        )
        return tile - (first + second)

    result = lax.map(
        one_group, (tiles, local_row.reshape(groups, 16), local_col.reshape(groups, 16))
    )
    return result.reshape(targets.shape)


def shards(diag_one, coupling, diag_two, off_one, off_two, targets, pattern):
    highest = lax.Precision.HIGHEST
    block = targets.shape[1]
    shard_blocks = off_one.shape[0] // block
    full_one, full_coupling, full_two = (
        lax.all_gather(diag_one, "row", axis=0, tiled=True),
        lax.all_gather(coupling, "row", axis=0, tiled=True),
        lax.all_gather(diag_two, "row", axis=0, tiled=True),
    )
    chol_one = jnp.linalg.cholesky(full_one)
    solve_one = make_solver(chol_one)
    lower_coupling = solve_one(full_coupling)
    lower_one = solve_one(off_one)
    schur = full_two - jnp.dot(lower_coupling, lower_coupling.T, precision=highest)
    chol_two = jnp.linalg.cholesky(schur)
    shifted = off_two - jnp.dot(lower_one, lower_coupling.T, precision=highest)
    lower_two = make_solver(chol_two)(shifted)
    row_one, row_two = (
        lax.all_gather(lower_one, "col", axis=0, tiled=True),
        lax.all_gather(lower_two, "col", axis=0, tiled=True),
    )
    col_one, col_two = (
        lax.all_gather(lower_one, "row", axis=0, tiled=True),
        lax.all_gather(lower_two, "row", axis=0, tiled=True),
    )
    updated = pair_updates(targets, pattern, row_one, row_two, col_one, col_two, shard_blocks)
    return (lower_one, lower_two, updated)


def solution(mesh):
    return jax.shard_map(
        shards,
        mesh=mesh,
        in_specs=(
            P("row", None),
            P("row", None),
            P("row", None),
            P(("row", "col"), None),
            P(("row", "col"), None),
            P(("row", "col"), None, None),
            P(("row", "col"), None),
        ),
        out_specs=(P(("row", "col"), None), P(("row", "col"), None), P(("row", "col"), None, None)),
        check_vma=False,
    )
```

profile of v0, /device:TPU:0, one launch (start us, length us, event | category | flops | bytes accessed | tf_op | source)
XLA Modules:
  0.0 922.9 jit_solution(18037836685526295646)
XLA Ops:
  9.4 45.8 %all-gather.8.cloned.1.call-done = f32[512,512]{1,0:T(8,128)} async-done(((f32[32,512]{1,0:T(8,128)}), f32[512,512]{1,0:T(8,128)}) %all-gather.8.cloned.1.call-update) | async-done | bytes 1048592 | tf_op jit(solution)/shard_map/all_gather | solution.py:55
  58.3 11.7 %cholesky.286 = f32[128,128]{1,0:T(8,128)S(1)} custom-call(f32[128,128]{1,0:T(8,128)S(1)} %cholesky.426), custom_call_target="Cholesky" | custom-call | tf_op jit(solution)/shard_map/jit(cholesky)/cholesky | solution.py:59
  70.0 9.8 %custom-call.31 = f32[1,128,128]{1,2,0:T(8,128)S(1)} custom-call(f32[1,128,128]{2,1,0:T(8,128)S(1)} %get-tuple-element.162), custom_call_target="InvertDiagBlocksLowerTriangular" | custom-call | tf_op jit(solution)/shard_map/jit(cholesky)/cholesky | solution.py:59
  80.7 11.7 %cholesky.305 = f32[128,128]{1,0:T(8,128)S(1)} custom-call(f32[128,128]{1,0:T(8,128)S(1)} %cholesky.430), custom_call_target="Cholesky" | custom-call | tf_op jit(solution)/shard_map/jit(cholesky)/cholesky | solution.py:59
  92.4 10.0 %custom-call.32 = f32[1,128,128]{1,2,0:T(8,128)S(1)} custom-call(f32[1,128,128]{2,1,0:T(8,128)S(1)} %get-tuple-element.159), custom_call_target="InvertDiagBlocksLowerTriangular" | custom-call | tf_op jit(solution)/shard_map/jit(cholesky)/cholesky | solution.py:59
  103.1 11.7 %cholesky.326 = f32[128,128]{1,0:T(8,128)S(1)} custom-call(f32[128,128]{1,0:T(8,128)S(1)} %cholesky.435), custom_call_target="Cholesky" | custom-call | tf_op jit(solution)/shard_map/jit(cholesky)/cholesky | solution.py:59
  115.5 9.8 %custom-call.33 = f32[1,128,128]{1,2,0:T(8,128)S(1)} custom-call(f32[1,128,128]{2,1,0:T(8,128)S(1)} %get-tuple-element.156), custom_call_target="InvertDiagBlocksLowerTriangular" | custom-call | tf_op jit(solution)/shard_map/jit(cholesky)/cholesky | solution.py:59
  125.9 11.7 %cholesky.343 = f32[128,128]{1,0:T(8,128)S(1)} custom-call(f32[128,128]{1,0:T(8,128)S(1)} %convolution_subtract_fusion.16), custom_call_target="Cholesky" | custom-call | tf_op jit(solution)/shard_map/jit(cholesky)/cholesky | solution.py:59
  141.5 10.3 %select_select_fusion.1 = f32[512,512]{1,0:T(8,128)S(1)} fusion(f32[512,512]{1,0:T(8,128)S(1)} %get-tuple-element.154, pred[]{:T(512)S(6)} %cholesky.348), kind=kLoop, calls=%fused_computation.25 | loop fusion | flops 1048576 | bytes 2097153 | tf_op jit(solution)/shard_map/triangular_solve/select.3 | solution.py:10
  151.9 8.0 while.16
  159.9 39.3 %custom-call.34 = f32[4,128,128]{1,2,0:T(8,128)S(1)} custom-call(f32[4,128,128]{2,1,0:T(8,128)S(1)} %get-tuple-element.75), custom_call_target="InvertDiagBlocksLowerTriangular" | custom-call | tf_op jit(solution)/shard_map/triangular_solve/custom-call.3 | solution.py:10
  215.2 11.7 %cholesky.358 = f32[128,128]{1,0:T(8,128)S(1)} custom-call(f32[128,128]{1,0:T(8,128)S(1)} %cholesky.439), custom_call_target="Cholesky" | custom-call | tf_op jit(solution)/shard_map/jit(cholesky)/cholesky | solution.py:64
  227.1 10.2 %custom-call.35 = f32[1,128,128]{1,2,0:T(8,128)S(1)} custom-call(f32[1,128,128]{2,1,0:T(8,128)S(1)} %get-tuple-element.152), custom_call_target="InvertDiagBlocksLowerTriangular" | custom-call | tf_op jit(solution)/shard_map/jit(cholesky)/cholesky | solution.py:64
  239.8 11.7 %cholesky.377 = f32[128,128]{1,0:T(8,128)S(1)} custom-call(f32[128,128]{1,0:T(8,128)S(1)} %cholesky.443), custom_call_target="Cholesky" | custom-call | tf_op jit(solution)/shard_map/jit(cholesky)/cholesky | solution.py:64
  252.9 9.8 %custom-call.36 = f32[1,128,128]{1,2,0:T(8,128)S(1)} custom-call(f32[1,128,128]{2,1,0:T(8,128)S(1)} %get-tuple-element.149), custom_call_target="InvertDiagBlocksLowerTriangular" | custom-call | tf_op jit(solution)/shard_map/jit(cholesky)/cholesky | solution.py:64
  265.9 13.2 %cholesky.398 = f32[128,128]{1,0:T(8,128)} custom-call(f32[128,128]{1,0:T(8,128)} %cholesky.448), custom_call_target="Cholesky" | custom-call | tf_op jit(solution)/shard_map/jit(cholesky)/cholesky | solution.py:64
  281.3 11.3 %custom-call.37 = f32[1,128,128]{1,2,0:T(8,128)} custom-call(f32[1,128,128]{2,1,0:T(8,128)} %get-tuple-element.146), custom_call_target="InvertDiagBlocksLowerTriangular" | custom-call | tf_op jit(solution)/shard_map/jit(cholesky)/cholesky | solution.py:64
  294.9 11.7 %cholesky.415 = f32[128,128]{1,0:T(8,128)S(1)} custom-call(f32[128,128]{1,0:T(8,128)S(1)} %convolution_subtract_fusion.15), custom_call_target="Cholesky" | custom-call | tf_op jit(solution)/shard_map/jit(cholesky)/cholesky | solution.py:64
  310.8 11.6 %while.17 = (s32[]{:T(128)}, f32[512,512]{1,0:T(8,128)}, s32[4,2]{0,1:T(2,128)S(1)}, f32[4,128,128]{2,1,0:T(8,128)S(1)}, s32[]{:T(128)}) while((s32[]{:T(128)}, f32[512,512]{1,0:T(8,128)}, s32[4,2]{0,1:T(2,128)S(1)}, f32[4,128,128]{2,1,0:T(8,128)S(1)}, s32[]{:T(128)}) %tuple.108), condition=%wide.while_cond.clone, body=%wide.while_body.clone.sunk | while | flops 2 | bytes 131181 | solution.py:10
  322.5 39.9 %custom-call.38 = f32[4,128,128]{1,2,0:T(8,128)} custom-call(f32[4,128,128]{2,1,0:T(8,128)S(1)} %get-tuple-element.76), custom_call_target="InvertDiagBlocksLowerTriangular" | custom-call | tf_op jit(solution)/shard_map/triangular_solve/custom-call.3 | solution.py:10
  384.6 24.9 %all-gather.18.cloned.1.call-done = f32[2048,512]{0,1:T(8,128)} async-done(((f32[256,512]{0,1:T(8,128)}), f32[2048,512]{0,1:T(8,128)}) %all-gather.18.cloned.1.call-update) | async-done | bytes 4194320 | tf_op jit(solution)/shard_map/all_gather | solution.py:69
  409.5 5.5 copy.34
  415.0 28.0 %all-gather.14.cloned.1.call-done = f32[2048,512]{0,1:T(8,128)} async-done(((f32[256,512]{0,1:T(8,128)}), f32[2048,512]{0,1:T(8,128)}) %all-gather.14.cloned.1.call-update) | async-done | bytes 4194320 | tf_op jit(solution)/shard_map/all_gather | solution.py:68
  443.1 5.4 copy.32
  448.4 73.9 %all-gather.20.cloned.1.call-done = f32[4096,512]{0,1:T(8,128)} async-done(((f32[256,512]{0,1:T(8,128)}), f32[4096,512]{0,1:T(8,128)}) %all-gather.20.cloned.1.call-update) | async-done | bytes 8388624 | tf_op jit(solution)/shard_map/all_gather | solution.py:73
  522.4 9.0 copy.35
  531.4 69.8 %all-gather.16.cloned.1.call-done = f32[4096,512]{0,1:T(8,128)} async-done(((f32[256,512]{0,1:T(8,128)}), f32[4096,512]{0,1:T(8,128)}) %all-gather.16.cloned.1.call-update) | async-done | bytes 8388624 | tf_op jit(solution)/shard_map/all_gather | solution.py:72
  601.1 9.0 copy.33
  610.1 305.6 %while.15 = (s32[]{:T(128)}, f32[8,16,128,128]{3,2,1,0:T(8,128)}, f32[8,16,128,128]{3,2,1,0:T(8,128)}, s32[8,16]{1,0:T(8,128)S(1)}, f32[16,128,512]{2,1,0:T(8,12...) while((s32[]{:T(128)}, f32[8,16,128,128]{3,2,1,0:T(8,128)}, ...), condition=%wide.region_9.12_spmd, body=%wide.region_8.11_spmd.sunk | while | flops 3221751808 | bytes 54535400 | solution.py:44
  610.1 4.9 gather_fusion
  615.1 6.2 gather_fusion.1
  621.2 7.4 fusion.128
  628.6 4.9 gather_fusion.2
  633.6 6.2 gather_fusion.3
  639.7 8.6 fusion.129
  653.3 6.2 gather_fusion.1
  659.4 7.4 fusion.128
  666.8 4.9 gather_fusion.2
  671.8 6.2 gather_fusion.3
  677.9 8.6 fusion.129
  691.4 6.2 gather_fusion.1
  697.6 7.4 fusion.128
  709.9 6.2 gather_fusion.3
  716.1 8.6 fusion.129
  729.6 6.2 gather_fusion.1
  735.8 7.4 fusion.128
  748.1 6.2 gather_fusion.3
  754.3 8.6 fusion.129
  767.8 6.2 gather_fusion.1
  774.0 7.4 fusion.128
  786.3 6.2 gather_fusion.3
  792.5 8.6 fusion.129
  806.0 6.2 gather_fusion.1
  812.2 7.4 fusion.128
  824.5 6.2 gather_fusion.3
  830.7 8.6 fusion.129
  844.2 6.2 gather_fusion.1
  850.4 7.4 fusion.128
  862.7 6.2 gather_fusion.3
  868.9 8.6 fusion.129
  882.4 6.2 gather_fusion.1
  888.6 7.4 fusion.128
  900.9 6.2 gather_fusion.3
  907.1 8.6 fusion.129
  (176 shorter events, 144.1 us)
Async XLA Ops:
  7.2 48.1 %all-gather.8.cloned.1.call-start = ((), (), s32[]{:S(2)}) async-start(), calls=%async_computation | async-start | bytes 1114112 | tf_op jit(solution)/shard_map/all_gather | solution.py:55
  7.9 191.4 %all-gather.12.cloned.1.call-start = ((), (), s32[]{:S(2)}) async-start(), calls=%async_computation.2 | async-start | bytes 1114112 | tf_op jit(solution)/shard_map/all_gather | solution.py:56
  8.6 200.2 %all-gather.10.cloned.1.call-start = ((), (), s32[]{:S(2)}) async-start(), calls=%async_computation.1 | async-start | bytes 1114112 | tf_op jit(solution)/shard_map/all_gather | solution.py:57
  9.4 400.1 %all-gather.18.cloned.1.call-start = ((), (), s32[]{:S(2)}) async-start(), calls=%async_computation.5 | async-start | bytes 4718592 | tf_op jit(solution)/shard_map/all_gather | solution.py:69
  199.2 9.6 %copy-start.5 = (f32[4,128,128]{1,2,0:T(8,128)}, f32[4,128,128]{1,2,0:T(8,128)S(1)}, u32[]{:S(2)}) copy-start(f32[4,128,128]{1,2,0:T(8,128)S(1)} %custom-call.34) | copy-start | bytes 786436
  202.7 2.5 copy-start
  205.2 2.5 copy-start.3
  214.2 1.0 copy-start.2
  215.2 147.3 %copy-start.6 = (f32[4,128,128]{1,2,0:T(8,128)S(1)}, f32[4,128,128]{1,2,0:T(8,128)}, u32[]{:S(2)}) copy-start(f32[4,128,128]{1,2,0:T(8,128)} %copy-done.5) | copy-start | bytes 786436
  239.8 22.9 %copy-start.8 = (f32[384,128]{1,0:T(8,128)}, f32[384,128]{1,0:T(8,128)S(1)}, u32[]{:S(2)}) copy-start(f32[384,128]{1,0:T(8,128)S(1)} %convolution_subtract_fusion.5) | copy-start | bytes 589828
  262.7 106.5 %copy-start.1 = (f32[512,128]{0,1:T(8,128)S(1)}, f32[512,128]{0,1:T(8,128)}, u32[]{:S(2)}) copy-start(f32[512,128]{0,1:T(8,128)} %copy-done) | copy-start | bytes 786436
  262.7 106.5 %copy-start.4 = (f32[512,128]{0,1:T(8,128)S(1)}, f32[512,128]{0,1:T(8,128)}, u32[]{:S(2)}) copy-start(f32[512,128]{0,1:T(8,128)} %copy-done.3) | copy-start | bytes 786436
  262.7 106.5 %copy-start.7 = (f32[512,128]{0,1:T(8,128)S(1)}, f32[512,128]{0,1:T(8,128)}, u32[]{:S(2)}) copy-start(f32[512,128]{0,1:T(8,128)} %fusion.75) | copy-start | bytes 786436
  362.4 8.9 copy-start.9
  371.4 8.9 copy-start.10
  378.0 65.0 %all-gather.14.cloned.1.call-start = ((), (), s32[]{:S(2)}) async-start(), calls=%async_computation.3 | async-start | bytes 4718592 | tf_op jit(solution)/shard_map/all_gather | solution.py:68
  378.9 143.4 %all-gather.20.cloned.1.call-start = ((), (), s32[]{:S(2)}) async-start(), calls=%async_computation.6 | async-start | bytes 8912896 | tf_op jit(solution)/shard_map/all_gather | solution.py:73
  379.5 221.6 %all-gather.16.cloned.1.call-start = ((), (), s32[]{:S(2)}) async-start(), calls=%async_computation.4 | async-start | bytes 8912896 | tf_op jit(solution)/shard_map/all_gather | solution.py:72
Sparse Core Ops, SparseCore 0:
  10.1 45.0 all-gather.7
  57.4 42.2 all-gather.11
  101.8 42.5 all-gather.9
  378.1 31.3 all-gather.17
  411.0 31.9 all-gather.13
  445.0 77.2 all-gather.19
  524.5 76.6 all-gather.15
where the time goes:
time: 934 us; the launch traced here: 923 us
  other arithmetic  257 us (28%)
  waiting for transfers between devices  246 us (26%)
  local copies, waits for them, and re-layouts  235 us (25%)
  matrix products  164 us (18%)
  between operations  20.2 us (2%)
    another operation x7, other arithmetic, apply_solve(): lax.linalg.triangular_solve(chol, rows, left_side=False, lower=True, tran...  92.4 us
    another operation x15, other arithmetic, shards(): chol_two = jnp.linalg.cholesky(schur)  83.8 us
    another operation x14, other arithmetic, shards(): chol_one = jnp.linalg.cholesky(full_one)  78.6 us
    all_gather x1, waiting for transfers between devices, shards(): lax.all_gather(lower_two, 'row', axis=0, tiled=True)  73.9 us
    all_gather x1, waiting for transfers between devices, shards(): lax.all_gather(lower_one, 'row', axis=0, tiled=True)  69.8 us
    dot_general x8, matrix products, one_group(): jnp.einsum('kaw,kbw->kab', row_blocks_two[row_id], col_blocks_two[col_id]...  68.7 us
    dot_general x8, matrix products, one_group(): jnp.einsum('kaw,kbw->kab', row_blocks_one[row_id], col_blocks_one[col_id]...  59.2 us
    gather x8, local copies, waits for them, and re-layouts, one_group(): col_blocks_one[col_id]  49.3 us
  transfers between devices with their start and end apart: 7, of which 5 were waited for; matrix products, arithmetic and copies ran while one was open for 19% of the time, Pallas kernels for 0%

commit v1 on v0

--- a/solution.py
+++ b/solution.py
@@ -1,7 +1,28 @@
+import functools
 import jax
 import jax.numpy as jnp
 from jax import lax
 from jax.sharding import PartitionSpec as P
+
+
+def change_signs(vector, d0):
+    world_n = lax.psum(1, axis_name="row")
+    samples = []
+    for i in range(world_n):
+        samples.append((i, (i + 1) % world_n))
+    nodes = []
+    for i in range(world_n):
+        nodes.append((i, (i - 1) % world_n))
+    n_now, top = ([vector], [vector])
+    for _ in range(world_n // 2):
+        n_now.append(lax.ppermute(n_now[-1], axis_name="row", perm=samples))
+    for _ in range((world_n - 1) // 2):
+        top.append(lax.ppermute(top[-1], axis_name="row", perm=nodes))
+    value_now = jnp.concatenate([*n_now[::-1], *top[1:]], axis=d0)
+    return jnp.roll(value_now, (lax.axis_index("row") - world_n // 2) * vector.shape[d0], d0)
+
+
+frame_order = functools.partial(change_signs, d0=0)
 
 
 def make_solver(chol):
@@ -69,7 +90,7 @@
         lax.all_gather(lower_two, "col", axis=0, tiled=True),
     )
     col_one, col_two = (
-        lax.all_gather(lower_one, "row", axis=0, tiled=True),
+        frame_order(lower_one),
         lax.all_gather(lower_two, "row", axis=0, tiled=True),
     )
     updated = pair_updates(targets, pattern, row_one, row_two, col_one, col_two, shard_blocks)

time: 934 us -> 858 us (0.919)
  waiting for transfers between devices: 246 us -> 122 us
  starting transfers between devices: 0.27 us -> 39.7 us
  local copies, waits for them, and re-layouts: 235 us -> 253 us
  other arithmetic: 257 us -> 242 us
  between operations: 20.2 us -> 30.6 us
    all_gather x1, waiting for transfers between devices: 73.9 us -> 3.24 us  [shards(): lax.all_gather(lower_two, 'row', axis=0, tiled=True)]
    ppermute x0 -> x15, waiting for transfers between devices: none -> 70 us  [the longest x8 62.7 us: change_signs(): n_now.append(lax.ppermute(n_now[-1], axis_name='row', perm=samples))]
    all_gather x1 -> x0, waiting for transfers between devices: 69.8 us -> none  [shards(): lax.all_gather(lower_one, 'row', axis=0, tiled=True)]
    ppermute x0 -> x15, starting transfers between devices: none -> 39.5 us  [the longest x7 38.2 us: change_signs(): top.append(lax.ppermute(top[-1], axis_name='row', perm=nodes))]
    all_gather x1, waiting for transfers between devices: 28 us -> 0.01 us  [shards(): lax.all_gather(lower_one, 'col', axis=0, tiled=True)]
    all_gather x1, waiting for transfers between devices: 24.9 us -> 0.01 us  [shards(): lax.all_gather(lower_two, 'col', axis=0, tiled=True)]
    unnamed x24 -> x59, local copies, waits for them, and re-layouts: 5.08 us -> 22.1 us
    dynamic_slice x0 -> x2, local copies, waits for them, and re-layouts: none -> 13.1 us  [change_signs(): jnp.roll(value_now, (lax.axis_index('row') - world_n // 2) * vector.shape...]
  transfers between devices with their start and end apart: 7 -> 21, of which waited for: 5 -> 11; matrix products, arithmetic and copies ran while one was open for 19% -> 23% of each run, Pallas kernels for 0% -> 0%
where the time goes in v1:
time: 858 us; the launch traced here: 846 us
  local copies, waits for them, and re-layouts  253 us (29%)
  other arithmetic  242 us (28%)
  matrix products  159 us (19%)
  waiting for transfers between devices  122 us (14%)
  starting transfers between devices  39.7 us (5%)
  between operations  30.6 us (4%)
    another operation x7, other arithmetic, apply_solve(): lax.linalg.triangular_solve(chol, rows, left_side=False, lower=True, tran...  80.8 us
    another operation x15, other arithmetic, shards(): chol_two = jnp.linalg.cholesky(schur)  79.5 us
    another operation x14, other arithmetic, shards(): chol_one = jnp.linalg.cholesky(full_one)  78.6 us
    dot_general x8, matrix products, one_group(): jnp.einsum('kaw,kbw->kab', row_blocks_two[row_id], col_blocks_two[col_id]...  68.7 us
    ppermute x8, waiting for transfers between devices, change_signs(): n_now.append(lax.ppermute(n_now[-1], axis_name='row', perm=samples))  62.7 us
    dot_general x8, matrix products, one_group(): jnp.einsum('kaw,kbw->kab', row_blocks_one[row_id], col_blocks_one[col_id]...  59.2 us
    gather x8, local copies, waits for them, and re-layouts, one_group(): col_blocks_one[col_id]  49.2 us
    gather x8, local copies, waits for them, and re-layouts, one_group(): col_blocks_two[col_id]  49.2 us
  transfers between devices with their start and end apart: 21, of which 11 were waited for; matrix products, arithmetic and copies ran while one was open for 23% of the time, Pallas kernels for 0%

profile of v1, /device:TPU:0, one launch (start us, length us, event | category | flops | bytes accessed | tf_op | source)
XLA Modules:
  0.0 846.0 jit_solution(13828524152370914763)
XLA Ops:
  9.4 45.8 %all-gather.7.cloned.1.call-done = f32[512,512]{1,0:T(8,128)} async-done(((f32[32,512]{1,0:T(8,128)}), f32[512,512]{1,0:T(8,128)}) %all-gather.7.cloned.1.call-update) | async-done | bytes 1048592 | tf_op jit(solution)/shard_map/all_gather | solution.py:76
  58.3 11.7 %cholesky.286 = f32[128,128]{1,0:T(8,128)S(1)} custom-call(f32[128,128]{1,0:T(8,128)S(1)} %cholesky.426), custom_call_target="Cholesky" | custom-call | tf_op jit(solution)/shard_map/jit(cholesky)/cholesky | solution.py:80
  70.0 9.8 %custom-call.31 = f32[1,128,128]{1,2,0:T(8,128)S(1)} custom-call(f32[1,128,128]{2,1,0:T(8,128)S(1)} %get-tuple-element.174), custom_call_target="InvertDiagBlocksLowerTriangular" | custom-call | tf_op jit(solution)/shard_map/jit(cholesky)/cholesky | solution.py:80
  80.7 11.7 %cholesky.305 = f32[128,128]{1,0:T(8,128)S(1)} custom-call(f32[128,128]{1,0:T(8,128)S(1)} %cholesky.430), custom_call_target="Cholesky" | custom-call | tf_op jit(solution)/shard_map/jit(cholesky)/cholesky | solution.py:80
  92.4 10.0 %custom-call.32 = f32[1,128,128]{1,2,0:T(8,128)S(1)} custom-call(f32[1,128,128]{2,1,0:T(8,128)S(1)} %get-tuple-element.171), custom_call_target="InvertDiagBlocksLowerTriangular" | custom-call | tf_op jit(solution)/shard_map/jit(cholesky)/cholesky | solution.py:80
  103.1 11.7 %cholesky.326 = f32[128,128]{1,0:T(8,128)S(1)} custom-call(f32[128,128]{1,0:T(8,128)S(1)} %cholesky.435), custom_call_target="Cholesky" | custom-call | tf_op jit(solution)/shard_map/jit(cholesky)/cholesky | solution.py:80
  115.5 9.8 %custom-call.33 = f32[1,128,128]{1,2,0:T(8,128)S(1)} custom-call(f32[1,128,128]{2,1,0:T(8,128)S(1)} %get-tuple-element.168), custom_call_target="InvertDiagBlocksLowerTriangular" | custom-call | tf_op jit(solution)/shard_map/jit(cholesky)/cholesky | solution.py:80
  125.9 11.7 %cholesky.343 = f32[128,128]{1,0:T(8,128)S(1)} custom-call(f32[128,128]{1,0:T(8,128)S(1)} %convolution_subtract_fusion.16), custom_call_target="Cholesky" | custom-call | tf_op jit(solution)/shard_map/jit(cholesky)/cholesky | solution.py:80
  151.8 8.0 while.16
  159.8 39.3 %custom-call.34 = f32[4,128,128]{1,2,0:T(8,128)S(1)} custom-call(f32[4,128,128]{2,1,0:T(8,128)S(1)} %get-tuple-element.75), custom_call_target="InvertDiagBlocksLowerTriangular" | custom-call | tf_op jit(solution)/shard_map/triangular_solve/custom-call.3 | solution.py:31
  221.3 12.1 %cholesky.358 = f32[128,128]{1,0:T(8,128)S(1)} custom-call(f32[128,128]{1,0:T(8,128)S(1)} %cholesky.439), custom_call_target="Cholesky" | custom-call | tf_op jit(solution)/shard_map/jit(cholesky)/cholesky | solution.py:85
  233.5 9.8 %custom-call.35 = f32[1,128,128]{1,2,0:T(8,128)S(1)} custom-call(f32[1,128,128]{2,1,0:T(8,128)S(1)} %get-tuple-element.164), custom_call_target="InvertDiagBlocksLowerTriangular" | custom-call | tf_op jit(solution)/shard_map/jit(cholesky)/cholesky | solution.py:85
  245.9 11.7 %cholesky.377 = f32[128,128]{1,0:T(8,128)S(1)} custom-call(f32[128,128]{1,0:T(8,128)S(1)} %cholesky.443), custom_call_target="Cholesky" | custom-call | tf_op jit(solution)/shard_map/jit(cholesky)/cholesky | solution.py:85
  258.9 9.8 %custom-call.36 = f32[1,128,128]{1,2,0:T(8,128)S(1)} custom-call(f32[1,128,128]{2,1,0:T(8,128)S(1)} %get-tuple-element.161), custom_call_target="InvertDiagBlocksLowerTriangular" | custom-call | tf_op jit(solution)/shard_map/jit(cholesky)/cholesky | solution.py:85
  270.3 11.9 %cholesky.398 = f32[128,128]{1,0:T(8,128)S(1)} custom-call(f32[128,128]{1,0:T(8,128)S(1)} %cholesky.448), custom_call_target="Cholesky" | custom-call | tf_op jit(solution)/shard_map/jit(cholesky)/cholesky | solution.py:85
  282.8 9.8 %custom-call.37 = f32[1,128,128]{1,2,0:T(8,128)S(1)} custom-call(f32[1,128,128]{2,1,0:T(8,128)S(1)} %get-tuple-element.158), custom_call_target="InvertDiagBlocksLowerTriangular" | custom-call | tf_op jit(solution)/shard_map/jit(cholesky)/cholesky | solution.py:85
  294.1 11.7 %cholesky.415 = f32[128,128]{1,0:T(8,128)S(1)} custom-call(f32[128,128]{1,0:T(8,128)S(1)} %convolution_subtract_fusion.15), custom_call_target="Cholesky" | custom-call | tf_op jit(solution)/shard_map/jit(cholesky)/cholesky | solution.py:85
  309.1 8.0 while.17
  317.2 39.5 %custom-call.38 = f32[4,128,128]{1,2,0:T(8,128)S(1)} custom-call(f32[4,128,128]{2,1,0:T(8,128)S(1)} %get-tuple-element.76), custom_call_target="InvertDiagBlocksLowerTriangular" | custom-call | tf_op jit(solution)/shard_map/triangular_solve/custom-call.3 | solution.py:31
  365.7 14.2 %collective-permute-done = f32[256,512]{0,1:T(8,128)S(1)} collective-permute-done((f32[256,512]{0,1:T(8,128)}, f32[256,512]{0,1:T(8,128)S(1)}, u32[]{:S(2)}, u32[]{:S(2)}) %collective-permute-start) | collective-permute-done | bytes 524320 | tf_op jit(solution)/shard_map/ppermute | solution.py:18
  385.2 9.0 %collective-permute-done.1 = f32[256,512]{0,1:T(8,128)S(1)} collective-permute-done((f32[256,512]{0,1:T(8,128)S(1)}, f32[256,512]{0,1:T(8,128)S(1)}, u32[]{:S(2)}, u32[]{:S(2)}) %collective-permute-start.1) | collective-permute-done | bytes 524320 | tf_op jit(solution)/shard_map/ppermute | solution.py:18
  399.6 8.1 collective-permute-done.2
  413.1 7.3 collective-permute-done.3
  426.5 7.0 collective-permute-done.4
  434.3 5.6 collective-permute-start.12
  439.9 9.3 %collective-permute-done.5 = f32[256,512]{0,1:T(8,128)S(1)} collective-permute-done((f32[256,512]{0,1:T(8,128)S(1)}, f32[256,512]{0,1:T(8,128)S(1)}, u32[]{:S(2)}, u32[]{:S(2)}) %collective-permute-start.5) | collective-permute-done | bytes 524320 | tf_op jit(solution)/shard_map/ppermute | solution.py:18
  449.2 7.3 collective-permute-done.12
  456.6 5.9 collective-permute-start.13
  500.4 9.3 %copy.35 = f32[4096,512]{1,0:T(8,128)} copy(f32[4096,512]{0,1:T(8,128)} %constant_dynamic-slice_fusion.4) | data formatting | bytes 16777216 | tf_op jit(solution)/shard_map/jit(_roll_dynamic)/dynamic_slice | solution.py:22
  509.7 5.5 copy.43
  523.8 9.0 %copy.44 = f32[4096,512]{1,0:T(8,128)} copy(f32[4096,512]{0,1:T(8,128)} %all-gather.17.cloned.1.call-done) | data formatting | bytes 16777216 | tf_op jit(solution)/shard_map/while | solution.py:65
  532.8 305.8 %while.15 = (s32[]{:T(128)}, f32[8,16,128,128]{3,2,1,0:T(8,128)}, f32[8,16,128,128]{3,2,1,0:T(8,128)}, s32[8,16]{1,0:T(8,128)S(1)}, f32[16,128,512]{2,1,0:T(8,12...) while((s32[]{:T(128)}, f32[8,16,128,128]{3,2,1,0:T(8,128)}, ...), condition=%wide.region_9.12_spmd, body=%wide.region_8.11_spmd.sunk | while | flops 3221751808 | bytes 54535400 | solution.py:65
  537.8 6.1 gather_fusion.1
  544.0 7.4 fusion.128
  556.4 6.1 gather_fusion.3
  562.5 8.6 %fusion.129 = f32[8,16,128,128]{3,2,1,0:T(8,128)} fusion(f32[8,16,128,128]{3,2,1,0:T(8,128)} %get-tuple-element.341, s32[]{:T(128)} %get-tuple-element.340, f32[16,128,128]{2,1,0:T(8,128)S(1)} %fusion.128, f32[16,128,512]{2,1,0:T(8,128)} %gather_fusion.2, f32[16,128,512]{2,1,0:T(8,128)} %gather_fusion.3, f32[8,16,128,128]{3,2,1,0:T(8,128)} %get-tuple-element.352), kind=kOutput, calls=%fused_computation.11.clone.1 | convolution fusion | flops 1611137024 | bytes 11534848 | tf_op jit(solution)/shard_map/while/body/eval_jaxpr/kaw,kbw->kab/dot_general | solution.py:60
  576.1 6.1 gather_fusion.1
  582.2 7.4 fusion.128
  594.6 6.1 gather_fusion.3
  600.7 8.6 %fusion.129 = f32[8,16,128,128]{3,2,1,0:T(8,128)} fusion(f32[8,16,128,128]{3,2,1,0:T(8,128)} %get-tuple-element.341, s32[]{:T(128)} %get-tuple-element.340, f32[16,128,128]{2,1,0:T(8,128)S(1)} %fusion.128, f32[16,128,512]{2,1,0:T(8,128)} %gather_fusion.2, f32[16,128,512]{2,1,0:T(8,128)} %gather_fusion.3, f32[8,16,128,128]{3,2,1,0:T(8,128)} %get-tuple-element.352), kind=kOutput, calls=%fused_computation.11.clone.1 | convolution fusion | flops 1611137024 | bytes 11534848 | tf_op jit(solution)/shard_map/while/body/eval_jaxpr/kaw,kbw->kab/dot_general | solution.py:60
  614.3 6.1 gather_fusion.1
  620.4 7.4 fusion.128
  632.8 6.1 gather_fusion.3
  639.0 8.6 %fusion.129 = f32[8,16,128,128]{3,2,1,0:T(8,128)} fusion(f32[8,16,128,128]{3,2,1,0:T(8,128)} %get-tuple-element.341, s32[]{:T(128)} %get-tuple-element.340, f32[16,128,128]{2,1,0:T(8,128)S(1)} %fusion.128, f32[16,128,512]{2,1,0:T(8,128)} %gather_fusion.2, f32[16,128,512]{2,1,0:T(8,128)} %gather_fusion.3, f32[8,16,128,128]{3,2,1,0:T(8,128)} %get-tuple-element.352), kind=kOutput, calls=%fused_computation.11.clone.1 | convolution fusion | flops 1611137024 | bytes 11534848 | tf_op jit(solution)/shard_map/while/body/eval_jaxpr/kaw,kbw->kab/dot_general | solution.py:60
  652.5 6.1 gather_fusion.1
  658.7 7.4 fusion.128
  671.0 6.1 gather_fusion.3
  677.2 8.6 %fusion.129 = f32[8,16,128,128]{3,2,1,0:T(8,128)} fusion(f32[8,16,128,128]{3,2,1,0:T(8,128)} %get-tuple-element.341, s32[]{:T(128)} %get-tuple-element.340, f32[16,128,128]{2,1,0:T(8,128)S(1)} %fusion.128, f32[16,128,512]{2,1,0:T(8,128)} %gather_fusion.2, f32[16,128,512]{2,1,0:T(8,128)} %gather_fusion.3, f32[8,16,128,128]{3,2,1,0:T(8,128)} %get-tuple-element.352), kind=kOutput, calls=%fused_computation.11.clone.1 | convolution fusion | flops 1611137024 | bytes 11534848 | tf_op jit(solution)/shard_map/while/body/eval_jaxpr/kaw,kbw->kab/dot_general | solution.py:60
  690.8 6.1 gather_fusion.1
  696.9 7.4 fusion.128
  709.3 6.1 gather_fusion.3
  715.4 8.6 %fusion.129 = f32[8,16,128,128]{3,2,1,0:T(8,128)} fusion(f32[8,16,128,128]{3,2,1,0:T(8,128)} %get-tuple-element.341, s32[]{:T(128)} %get-tuple-element.340, f32[16,128,128]{2,1,0:T(8,128)S(1)} %fusion.128, f32[16,128,512]{2,1,0:T(8,128)} %gather_fusion.2, f32[16,128,512]{2,1,0:T(8,128)} %gather_fusion.3, f32[8,16,128,128]{3,2,1,0:T(8,128)} %get-tuple-element.352), kind=kOutput, calls=%fused_computation.11.clone.1 | convolution fusion | flops 1611137024 | bytes 11534848 | tf_op jit(solution)/shard_map/while/body/eval_jaxpr/kaw,kbw->kab/dot_general | solution.py:60
  729.0 6.1 gather_fusion.1
  735.1 7.4 fusion.128
  747.5 6.1 gather_fusion.3
  753.6 8.6 %fusion.129 = f32[8,16,128,128]{3,2,1,0:T(8,128)} fusion(f32[8,16,128,128]{3,2,1,0:T(8,128)} %get-tuple-element.341, s32[]{:T(128)} %get-tuple-element.340, f32[16,128,128]{2,1,0:T(8,128)S(1)} %fusion.128, f32[16,128,512]{2,1,0:T(8,128)} %gather_fusion.2, f32[16,128,512]{2,1,0:T(8,128)} %gather_fusion.3, f32[8,16,128,128]{3,2,1,0:T(8,128)} %get-tuple-element.352), kind=kOutput, calls=%fused_computation.11.clone.1 | convolution fusion | flops 1611137024 | bytes 11534848 | tf_op jit(solution)/shard_map/while/body/eval_jaxpr/kaw,kbw->kab/dot_general | solution.py:60
  767.2 6.1 gather_fusion.1
  773.4 7.4 fusion.128
  785.7 6.1 gather_fusion.3
  791.9 8.6 %fusion.129 = f32[8,16,128,128]{3,2,1,0:T(8,128)} fusion(f32[8,16,128,128]{3,2,1,0:T(8,128)} %get-tuple-element.341, s32[]{:T(128)} %get-tuple-element.340, f32[16,128,128]{2,1,0:T(8,128)S(1)} %fusion.128, f32[16,128,512]{2,1,0:T(8,128)} %gather_fusion.2, f32[16,128,512]{2,1,0:T(8,128)} %gather_fusion.3, f32[8,16,128,128]{3,2,1,0:T(8,128)} %get-tuple-element.352), kind=kOutput, calls=%fused_computation.11.clone.1 | convolution fusion | flops 1611137024 | bytes 11534848 | tf_op jit(solution)/shard_map/while/body/eval_jaxpr/kaw,kbw->kab/dot_general | solution.py:60
  805.4 6.1 gather_fusion.1
  811.6 7.4 fusion.128
  824.0 6.1 gather_fusion.3
  830.1 8.6 %fusion.129 = f32[8,16,128,128]{3,2,1,0:T(8,128)} fusion(f32[8,16,128,128]{3,2,1,0:T(8,128)} %get-tuple-element.341, s32[]{:T(128)} %get-tuple-element.340, f32[16,128,128]{2,1,0:T(8,128)S(1)} %fusion.128, f32[16,128,512]{2,1,0:T(8,128)} %gather_fusion.2, f32[16,128,512]{2,1,0:T(8,128)} %gather_fusion.3, f32[8,16,128,128]{3,2,1,0:T(8,128)} %get-tuple-element.352), kind=kOutput, calls=%fused_computation.11.clone.1 | convolution fusion | flops 1611137024 | bytes 11534848 | tf_op jit(solution)/shard_map/while/body/eval_jaxpr/kaw,kbw->kab/dot_general | solution.py:60
  (242 shorter events, 213.5 us)
Async XLA Ops:
  7.2 48.1 %all-gather.7.cloned.1.call-start = ((), (), s32[]{:S(2)}) async-start(), calls=%async_computation | async-start | bytes 1114112 | tf_op jit(solution)/shard_map/all_gather | solution.py:76
  7.9 198.0 %all-gather.11.cloned.1.call-start = ((), (), s32[]{:S(2)}) async-start(), calls=%async_computation.2 | async-start | bytes 1114112 | tf_op jit(solution)/shard_map/all_gather | solution.py:77
  8.6 206.6 %all-gather.9.cloned.1.call-start = ((), (), s32[]{:S(2)}) async-start(), calls=%async_computation.1 | async-start | bytes 1114112 | tf_op jit(solution)/shard_map/all_gather | solution.py:78
  9.4 500.4 %all-gather.15.cloned.1.call-start = ((), (), s32[]{:S(2)}) async-start(), calls=%async_computation.4 | async-start | bytes 4718592 | tf_op jit(solution)/shard_map/all_gather | solution.py:90
  205.9 157.9 %copy-start.11 = (f32[256,128]{0,1:T(8,128)}, f32[256,128]{0,1:T(8,128)S(1)}, u32[]{:S(2)}) copy-start(f32[256,128]{0,1:T(8,128)S(1)} %fusion.76) | copy-start | bytes 393220
  208.9 258.3 %copy-start.13 = (s32[128,2]{0,1:T(2,128)S(1)}, s32[128,2]{0,1:T(2,128)}, u32[]{:S(2)}) copy-start(s32[128,2]{0,1:T(2,128)} %param.18) | copy-start | bytes 3076
  220.3 1.0 copy-start
  362.9 152.3 %all-gather.13.cloned.1.call-start = ((), (), s32[]{:S(2)}) async-start(), calls=%async_computation.3 | async-start | bytes 4718592 | tf_op jit(solution)/shard_map/all_gather | solution.py:89
  363.8 130.2 %copy-start.12 = (f32[256,128]{0,1:T(8,128)S(1)}, f32[256,128]{0,1:T(8,128)}, u32[]{:S(2)}) copy-start(f32[256,128]{0,1:T(8,128)} %copy-done.11) | copy-start | bytes 393220
  363.8 160.0 %all-gather.17.cloned.1.call-start = ((), (), s32[]{:S(2)}) async-start(), calls=%async_computation.5 | async-start | bytes 8912896 | tf_op jit(solution)/shard_map/all_gather | solution.py:94
  364.4 15.5 %collective-permute-start = (f32[256,512]{0,1:T(8,128)}, f32[256,512]{0,1:T(8,128)S(1)}, u32[]{:S(2)}, u32[]{:S(2)}) collective-permute-start(f32[256,512]{0,1:T(8,128)} %pad_maximum_fusion.3), channel_id=1, source_target_pairs={{0,8},{8,16},{16,24},{24,32},{32,40},{40,48},{48,56},{56,64},{64,7... | collective-permute-start | bytes 1572872 | tf_op jit(solution)/shard_map/ppermute | solution.py:18
  379.9 14.3 %collective-permute-start.1 = (f32[256,512]{0,1:T(8,128)S(1)}, f32[256,512]{0,1:T(8,128)S(1)}, u32[]{:S(2)}, u32[]{:S(2)}) collective-permute-start(f32[256,512]{0,1:T(8,128)S(1)} %collective-permute-done), channel_id=1, source_target_pairs={{0,8},{8,16},{16,24},{24,32},{32,40},{40,48},{48,56},{56,64},{64,7... | collective-permute-start | bytes 1572872 | tf_op jit(solution)/shard_map/ppermute | solution.py:18
  379.9 14.3 %collective-permute-start.8 = (f32[256,512]{0,1:T(8,128)}, f32[256,512]{0,1:T(8,128)S(1)}, u32[]{:S(2)}, u32[]{:S(2)}) collective-permute-start(f32[256,512]{0,1:T(8,128)} %pad_maximum_fusion.3), channel_id=1, source_target_pairs={{0,120},{8,0},{16,8},{24,16},{32,24},{40,32},{48,40},{56,48},{64,5... | collective-permute-start | bytes 1572872 | tf_op jit(solution)/shard_map/ppermute | solution.py:20
  394.2 13.5 %collective-permute-start.2 = (f32[256,512]{0,1:T(8,128)S(1)}, f32[256,512]{0,1:T(8,128)S(1)}, u32[]{:S(2)}, u32[]{:S(2)}) collective-permute-start(f32[256,512]{0,1:T(8,128)S(1)} %collective-permute-done.1), channel_id=1, source_target_pairs={{0,8},{8,16},{16,24},{24,32},{32,40},{40,48},{48,56},{56,64},{64,7... | collective-permute-start | bytes 1572872 | tf_op jit(solution)/shard_map/ppermute | solution.py:18
  394.2 13.5 %collective-permute-start.9 = (f32[256,512]{0,1:T(8,128)S(1)}, f32[256,512]{0,1:T(8,128)S(1)}, u32[]{:S(2)}, u32[]{:S(2)}) collective-permute-start(f32[256,512]{0,1:T(8,128)S(1)} %collective-permute-done.8), channel_id=1, source_target_pairs={{0,120},{8,0},{16,8},{24,16},{32,24},{40,32},{48,40},{56,48},{64,5... | collective-permute-start | bytes 1572872 | tf_op jit(solution)/shard_map/ppermute | solution.py:20
  407.7 12.6 %collective-permute-start.3 = (f32[256,512]{0,1:T(8,128)S(1)}, f32[256,512]{0,1:T(8,128)S(1)}, u32[]{:S(2)}, u32[]{:S(2)}) collective-permute-start(f32[256,512]{0,1:T(8,128)S(1)} %collective-permute-done.2), channel_id=1, source_target_pairs={{0,8},{8,16},{16,24},{24,32},{32,40},{40,48},{48,56},{56,64},{64,7... | collective-permute-start | bytes 1572872 | tf_op jit(solution)/shard_map/ppermute | solution.py:18
  407.7 12.6 %collective-permute-start.10 = (f32[256,512]{0,1:T(8,128)S(1)}, f32[256,512]{0,1:T(8,128)S(1)}, u32[]{:S(2)}, u32[]{:S(2)}) collective-permute-start(f32[256,512]{0,1:T(8,128)S(1)} %collective-permute-done.9), channel_id=1, source_target_pairs={{0,120},{8,0},{16,8},{24,16},{32,24},{40,32},{48,40},{56,48},{64,5... | collective-permute-start | bytes 1572872 | tf_op jit(solution)/shard_map/ppermute | solution.py:20
  420.3 36.2 %copy-start.5 = (f32[256,512]{0,1:T(8,128)}, f32[256,512]{0,1:T(8,128)S(1)}, u32[]{:S(2)}) copy-start(f32[256,512]{0,1:T(8,128)S(1)} %collective-permute-done.3) | copy-start | bytes 1572868
  420.3 13.1 %collective-permute-start.4 = (f32[256,512]{0,1:T(8,128)S(1)}, f32[256,512]{0,1:T(8,128)S(1)}, u32[]{:S(2)}, u32[]{:S(2)}) collective-permute-start(f32[256,512]{0,1:T(8,128)S(1)} %collective-permute-done.3), channel_id=1, source_target_pairs={{0,8},{8,16},{16,24},{24,32},{32,40},{40,48},{48,56},{56,64},{64,7... | collective-permute-start | bytes 1572872 | tf_op jit(solution)/shard_map/ppermute | solution.py:18
  420.4 0.8 copy-start.1
  421.2 12.3 %collective-permute-start.11 = (f32[256,512]{0,1:T(8,128)S(1)}, f32[256,512]{0,1:T(8,128)S(1)}, u32[]{:S(2)}, u32[]{:S(2)}) collective-permute-start(f32[256,512]{0,1:T(8,128)S(1)} %collective-permute-done.10), channel_id=1, source_target_pairs={{0,120},{8,0},{16,8},{24,16},{32,24},{40,32},{48,40},{56,48},{64,5... | collective-permute-start | bytes 1572872 | tf_op jit(solution)/shard_map/ppermute | solution.py:20
  433.5 29.0 %copy-start.7 = (f32[256,512]{0,1:T(8,128)}, f32[256,512]{0,1:T(8,128)S(1)}, u32[]{:S(2)}) copy-start(f32[256,512]{0,1:T(8,128)S(1)} %collective-permute-done.4) | copy-start | bytes 1572868
  433.5 15.8 %collective-permute-start.5 = (f32[256,512]{0,1:T(8,128)S(1)}, f32[256,512]{0,1:T(8,128)S(1)}, u32[]{:S(2)}, u32[]{:S(2)}) collective-permute-start(f32[256,512]{0,1:T(8,128)S(1)} %collective-permute-done.4), channel_id=1, source_target_pairs={{0,8},{8,16},{16,24},{24,32},{32,40},{40,48},{48,56},{56,64},{64,7... | collective-permute-start | bytes 1572872 | tf_op jit(solution)/shard_map/ppermute | solution.py:18
  433.5 0.9 copy-start.3
  434.3 22.2 %collective-permute-start.12 = (f32[256,512]{0,1:T(8,128)S(1)}, f32[256,512]{0,1:T(8,128)}, u32[]{:S(2)}, u32[]{:S(2)}) collective-permute-start(f32[256,512]{0,1:T(8,128)S(1)} %collective-permute-done.11), channel_id=1, source_target_pairs={{0,120},{8,0},{16,8},{24,16},{32,24},{40,32},{48,40},{56,48},{64,5... | collective-permute-start | bytes 1572872 | tf_op jit(solution)/shard_map/ppermute | solution.py:20
  449.2 17.9 %copy-start.9 = (f32[256,512]{0,1:T(8,128)}, f32[256,512]{0,1:T(8,128)S(1)}, u32[]{:S(2)}) copy-start(f32[256,512]{0,1:T(8,128)S(1)} %collective-permute-done.5) | copy-start | bytes 1572868
  449.2 17.9 %collective-permute-start.6 = (f32[256,512]{0,1:T(8,128)S(1)}, f32[256,512]{0,1:T(8,128)}, u32[]{:S(2)}, u32[]{:S(2)}) collective-permute-start(f32[256,512]{0,1:T(8,128)S(1)} %collective-permute-done.5), channel_id=1, source_target_pairs={{0,8},{8,16},{16,24},{24,32},{32,40},{40,48},{48,56},{56,64},{64,7... | collective-permute-start | bytes 1572872 | tf_op jit(solution)/shard_map/ppermute | solution.py:18
  456.6 14.9 %collective-permute-start.13 = (f32[256,512]{0,1:T(8,128)}, f32[256,512]{0,1:T(8,128)}, u32[]{:S(2)}, u32[]{:S(2)}) collective-permute-start(f32[256,512]{0,1:T(8,128)} %collective-permute-done.12), channel_id=1, source_target_pairs={{0,120},{8,0},{16,8},{24,16},{32,24},{40,32},{48,40},{56,48},{64,5... | collective-permute-start | bytes 1572872 | tf_op jit(solution)/shard_map/ppermute | solution.py:20
  467.1 12.8 %collective-permute-start.7 = (f32[256,512]{0,1:T(8,128)}, f32[256,512]{0,1:T(8,128)}, u32[]{:S(2)}, u32[]{:S(2)}) collective-permute-start(f32[256,512]{0,1:T(8,128)} %collective-permute-done.6), channel_id=1, source_target_pairs={{0,8},{8,16},{16,24},{24,32},{32,40},{40,48},{48,56},{56,64},{64,7... | collective-permute-start | bytes 1572872 | tf_op jit(solution)/shard_map/ppermute | solution.py:18
  471.4 22.2 %copy-start.10 = (f32[256,512]{0,1:T(8,128)S(1)}, f32[256,512]{0,1:T(8,128)}, u32[]{:S(2)}) copy-start(f32[256,512]{0,1:T(8,128)} %copy-done.9) | copy-start | bytes 1572868
  471.4 22.2 %copy-start.8 = (f32[256,512]{0,1:T(8,128)S(1)}, f32[256,512]{0,1:T(8,128)}, u32[]{:S(2)}) copy-start(f32[256,512]{0,1:T(8,128)} %copy-done.7) | copy-start | bytes 1572868
  471.4 22.3 %copy-start.6 = (f32[256,512]{0,1:T(8,128)S(1)}, f32[256,512]{0,1:T(8,128)}, u32[]{:S(2)}) copy-start(f32[256,512]{0,1:T(8,128)} %copy-done.5) | copy-start | bytes 1572868
  471.4 22.8 %copy-start.2 = (f32[256,512]{0,1:T(8,128)S(1)}, f32[256,512]{0,1:T(8,128)}, u32[]{:S(2)}) copy-start(f32[256,512]{0,1:T(8,128)} %copy-done.1) | copy-start | bytes 1572868
  471.4 22.9 %copy-start.4 = (f32[256,512]{0,1:T(8,128)S(1)}, f32[256,512]{0,1:T(8,128)}, u32[]{:S(2)}) copy-start(f32[256,512]{0,1:T(8,128)} %copy-done.3) | copy-start | bytes 1572868
  471.5 19.9 %collective-permute-start.14 = (f32[256,512]{0,1:T(8,128)}, f32[256,512]{0,1:T(8,128)S(1)}, u32[]{:S(2)}, u32[]{:S(2)}) collective-permute-start(f32[256,512]{0,1:T(8,128)} %collective-permute-done.13), channel_id=1, source_target_pairs={{0,120},{8,0},{16,8},{24,16},{32,24},{40,32},{48,40},{56,48},{64,5... | collective-permute-start | bytes 1572872 | tf_op jit(solution)/shard_map/ppermute | solution.py:20
Sparse Core Ops, SparseCore 0:
  10.1 45.0 all-gather.6
  57.4 42.2 all-gather.10
  101.8 42.4 all-gather.8
  363.0 31.3 all-gather.14
  395.9 31.9 all-gather.12
  429.9 93.8 all-gather.16
